TPU v7x, 128 devices: a whole 4x4x4 slice. The times are simulated.
128 devices in a mesh: section: 2 (over core), dp: 4 (over x), mp: 16 (over z, y).
Axes of the slice: x: 4, y: 4, z: 4, core: 2. Of those that a mesh axis runs over, the one named last changes fastest.
Arguments:
- segment_input: bfloat16 [2, 4, 256, 2048], P(None, 'dp', None, 'mp'), may hold values from -6 to 6
- out_grad: bfloat16 [2, 4, 256, 2048], P(None, 'dp', None, 'mp'), may hold values from -6 to 6
- pool_tokens: bfloat16 [16, 4, 128, 896], P('section', 'dp'), may hold values from -6 to 6
- neighbour_ids: int32 [2, 4, 4, 4], P(None, 'dp'), may hold values from 0 to 15, as said below
- neighbour_counts: int32 [2, 4, 4], P(None, 'dp'), may hold values from 1 to 4
- enc_gain: float32 [896], replicated, may hold values from 0.5 to 1.5
- enc_up: bfloat16 [896, 4096], P(None, 'mp'), may hold values from -0.1875 to 0.1875
- enc_down: bfloat16 [4096, 896], P(None, 'mp'), may hold values from -0.09375 to 0.09375
- norm_gain: float32 [2, 2048], P('section'), may hold values from 0.5 to 1.5
- w_query: bfloat16 [2, 2048, 4096], P('section', None, 'mp'), may hold values from -0.125 to 0.125
- w_key: bfloat16 [2, 896, 4096], P('section', None, 'mp'), may hold values from -0.1875 to 0.1875
- w_value: bfloat16 [2, 896, 4096], P('section', None, 'mp'), may hold values from -0.1875 to 0.1875
- w_out: bfloat16 [2, 4096, 2048], P('section', None, 'mp'), may hold values from -0.09375 to 0.09375
Outputs:
- grad_key: bfloat16 [2, 896, 4096], P('section', None, 'mp')
- grad_value: bfloat16 [2, 896, 4096], P('section', None, 'mp')
Inputs may be any that keep to these rules, and one draw needn't show every extreme that they name: `neighbour_ids`: the 4 slots of one stretch name distinct pool stretches.
All inputs are finite; a program needn't handle non-finite values.
Results may differ from a plain program's by a relative error of at most 0.025.
Values may be sent and summed in bfloat16 or wider, within the bound.
A program may use at most 128 MiB of HBM per device.

v0:
```python
import jax
import jax.numpy as jnp
from jax import lax
from jax.sharding import PartitionSpec as P

HEAD = 128
NT = 128
EPSILON = 1e-05


def passed_along(value, axis, by):
    peers = lax.axis_size(axis)
    pairs = [(i, i + by) for i in range(peers) if 0 <= i + by < peers]
    return lax.ppermute(value, axis, pairs)


def rms_scale(values):
    return lax.rsqrt(jnp.mean(values * values, axis=-1, keepdims=True) + EPSILON)


def collect(tensor):
    return lax.all_gather(tensor, "mp", axis=1, tiled=True)


def collect_pair(first, second):
    return (
        lax.all_gather(first, "mp", axis=1, tiled=True),
        lax.all_gather(second, "mp", axis=1, tiled=True),
    )


def pass_on(tensor, offset):
    return passed_along(tensor, "section", offset)


def attend(queries, key_block, value_block, usable):
    scores = jnp.einsum("cqhe,ckhe->chqk", queries, key_block, preferred_element_type=jnp.float32)
    scores = jnp.where(usable[:, None, None, :], scores, -1e30)
    weights = jax.nn.softmax(scores, axis=-1)
    weights_bf = weights.astype(jnp.bfloat16)
    attended = jnp.einsum(
        "chqk,ckhe->cqhe", weights_bf, value_block, preferred_element_type=jnp.float32
    )
    return (weights, weights_bf, attended.astype(jnp.bfloat16))


def attend_back(queries, key_block, value_block, weights, weights_bf, grad_attended):
    grad_weights = jnp.einsum(
        "cqhe,ckhe->chqk", grad_attended, value_block, preferred_element_type=jnp.float32
    )
    grad_scores = weights * (grad_weights - jnp.sum(weights * grad_weights, axis=-1, keepdims=True))
    grad_values = jnp.einsum(
        "chqk,cqhe->ckhe", weights_bf, grad_attended, preferred_element_type=jnp.float32
    ).astype(jnp.bfloat16)
    grad_keys = jnp.einsum("chqk,cqhe->ckhe", grad_scores, queries.astype(jnp.float32)).astype(
        jnp.bfloat16
    )
    grad_queries = jnp.einsum("chqk,ckhe->cqhe", grad_scores, key_block.astype(jnp.float32))
    return (grad_keys, grad_values, grad_queries)


def front(rows_in, gain_full, query_cols, key_block, value_block, usable, head_count):
    rows_wide = rows_in.astype(jnp.float32)
    inv_rms = rms_scale(rows_wide)
    normed = (rows_wide * inv_rms * gain_full).astype(jnp.bfloat16)
    query_raw = jnp.dot(normed, query_cols, preferred_element_type=jnp.float32)
    queries = (query_raw * HEAD ** (-0.5)).astype(jnp.bfloat16)
    queries = queries.reshape(key_block.shape[0], -1, head_count, HEAD)
    weights, weights_bf, attended = attend(queries, key_block, value_block, usable)
    return (inv_rms, query_raw, queries, weights, weights_bf, attended)


def on_device(
    segment_input,
    out_grad,
    pool_tokens,
    neighbour_ids,
    neighbour_counts,
    enc_gain,
    enc_up,
    enc_down,
    norm_gain,
    w_query,
    w_key,
    w_value,
    w_out,
):
    model_count = lax.axis_size("mp")
    model_index = lax.axis_index("mp")
    segment_count = lax.axis_size("section")
    segment_index = lax.axis_index("section")
    micro_count = segment_input.shape[0]
    row_count = segment_input.shape[2]
    feat_count = segment_input.shape[3]
    width = feat_count * model_count
    head_count = w_query.shape[2] // HEAD
    tract_count = neighbour_ids.shape[2]
    key_span = neighbour_ids.shape[3] * NT
    raw_rows = pool_tokens[:, 0].reshape(-1, pool_tokens.shape[3])
    raw_wide = raw_rows.astype(jnp.float32)
    enc_normed = (raw_wide * rms_scale(raw_wide) * enc_gain).astype(jnp.bfloat16)
    hidden_part = jax.nn.gelu(
        jnp.dot(enc_normed, enc_up, preferred_element_type=jnp.float32)
    ).astype(jnp.bfloat16)
    hidden_full = collect(hidden_part)
    enc_feat = enc_down.shape[1]
    raw_slice = lax.dynamic_slice_in_dim(raw_wide, model_index * enc_feat, enc_feat, 1)
    encoded = (
        raw_slice + jnp.dot(hidden_full, enc_down, preferred_element_type=jnp.float32)
    ).astype(jnp.bfloat16)
    slot_ids = neighbour_ids[:, 0].reshape(-1)
    shard_rows = encoded.shape[0]
    token_index = jnp.arange(NT, dtype=jnp.int32)
    global_rows = ((slot_ids * NT)[:, None] + token_index[None, :]).reshape(-1)
    empty_pool = jnp.zeros((segment_count * shard_rows, enc_feat * model_count), jnp.bfloat16)
    portion = lax.all_gather(encoded, ("section", "mp"), axis=0, tiled=True)
    shard_total = portion.shape[0] // shard_rows

    def one_shard(position, whole_pool):
        shard_block = lax.dynamic_slice_in_dim(portion, position * shard_rows, shard_rows, 0)
        row_start = position // model_count * shard_rows
        col_start = position % model_count * enc_feat
        return lax.dynamic_update_slice(whole_pool, shard_block, (row_start, col_start))

    whole_pool = lax.fori_loop(0, shard_total, one_shard, empty_pool)
    neighbours = jnp.take(whole_pool, global_rows, axis=0)

    def project(weight):
        projected = jnp.dot(neighbours, weight[0], preferred_element_type=jnp.float32).astype(
            jnp.bfloat16
        )
        return projected.reshape(micro_count, tract_count, key_span, head_count, HEAD)

    key_all = project(w_key)
    value_all = project(w_value)
    span_index = jnp.arange(key_span, dtype=jnp.int32) // NT
    usable_all = span_index[None, None, :] < neighbour_counts[:, 0][:, :, None]
    query_cols = w_query[0]
    out_cols = w_out[0]
    query_rows, out_rows = (
        lax.all_to_all(query_cols, "mp", split_axis=0, concat_axis=1, tiled=True),
        lax.all_to_all(out_cols, "mp", split_axis=0, concat_axis=1, tiled=True),
    )
    gain_full = norm_gain[0]
    gain_own = lax.dynamic_slice_in_dim(gain_full, model_index * feat_count, feat_count, 0)
    inputs_own = segment_input[:, 0]
    grads_own = out_grad[:, 0]
    step_count = micro_count + segment_count - 1
    empty_share = jnp.zeros((row_count, feat_count), jnp.bfloat16)
    stored_start = jnp.zeros((micro_count, row_count, width), jnp.bfloat16)

    def forward_step(step, state):
        received, stored = state
        which = step - segment_index
        active = (which >= 0) & (which < micro_count)
        which = jnp.clip(which, 0, micro_count - 1)
        incoming = jnp.where(segment_index == 0, inputs_own[which], received)
        rows_full = collect(incoming)
        outputs = front(
            rows_full,
            gain_full,
            query_cols,
            key_all[which],
            value_all[which],
            usable_all[which],
            head_count,
        )
        attended = collect(outputs[5].reshape(row_count, -1))
        result = incoming.astype(jnp.float32) + jnp.dot(
            attended, out_cols, preferred_element_type=jnp.float32
        )
        stored = stored.at[which].set(jnp.where(active, rows_full, stored[which]))
        return (pass_on(result.astype(jnp.bfloat16), 1), stored)

    _, stored = lax.fori_loop(0, step_count, forward_step, (empty_share, stored_start))
    grad_start = jnp.zeros((micro_count, tract_count, key_span, head_count, HEAD), jnp.bfloat16)

    def backward_step(step, state):
        received, key_grads, value_grads = state
        which = step - (segment_count - 1 - segment_index)
        active = (which >= 0) & (which < micro_count)
        which = jnp.clip(which, 0, micro_count - 1)
        incoming = jnp.where(segment_index == segment_count - 1, grads_own[which], received)
        rows_full = stored[which]
        rows_own = lax.dynamic_slice_in_dim(rows_full, model_index * feat_count, feat_count, 1)
        key_block = key_all[which]
        value_block = value_all[which]
        inv_rms, query_raw, queries, weights, weights_bf, _ = front(
            rows_full, gain_full, query_cols, key_block, value_block, usable_all[which], head_count
        )
        grad_full = collect(incoming)
        grad_att = jnp.dot(grad_full, out_rows.T, preferred_element_type=jnp.float32).astype(
            jnp.bfloat16
        )
        grad_att = grad_att.reshape(queries.shape)
        grad_keys, grad_values, grad_queries = attend_back(
            queries, key_block, value_block, weights, weights_bf, grad_att
        )
        grad_scaled = (grad_queries * HEAD ** (-0.5)).reshape(row_count, -1).astype(jnp.bfloat16)
        part_total = jnp.sum(
            grad_scaled.astype(jnp.float32) * query_raw, axis=1, keepdims=True
        ).astype(jnp.bfloat16)
        scaled_full, totals = collect_pair(grad_scaled, part_total)
        row_total = jnp.sum(totals.astype(jnp.float32), axis=1, keepdims=True)
        grad_normed = jnp.dot(scaled_full, query_rows.T, preferred_element_type=jnp.float32)
        rows_wide = rows_own.astype(jnp.float32)
        grad_in = (
            incoming.astype(jnp.float32)
            + inv_rms * gain_own * grad_normed
            - rows_wide * inv_rms * inv_rms * row_total / width
        )
        key_grads = key_grads.at[which].set(jnp.where(active, grad_keys, key_grads[which]))
        value_grads = value_grads.at[which].set(jnp.where(active, grad_values, value_grads[which]))
        return (pass_on(grad_in.astype(jnp.bfloat16), -1), key_grads, value_grads)

    _, key_grads, value_grads = lax.fori_loop(
        0, step_count, backward_step, (empty_share, grad_start, grad_start)
    )
    contract = (((0,), (0,)), ((), ()))
    key_sum = lax.dot_general(
        neighbours,
        key_grads.reshape(-1, head_count * HEAD),
        contract,
        preferred_element_type=jnp.float32,
    )
    value_sum = lax.dot_general(
        neighbours,
        value_grads.reshape(-1, head_count * HEAD),
        contract,
        preferred_element_type=jnp.float32,
    )
    key_total, value_total = (
        lax.psum(key_sum.astype(jnp.bfloat16), "dp").astype(jnp.float32),
        lax.psum(value_sum.astype(jnp.bfloat16), "dp").astype(jnp.float32),
    )
    return (key_total.astype(jnp.bfloat16)[None], value_total.astype(jnp.bfloat16)[None])


def solution(mesh):
    placed = (
        P(None, "dp", None, "mp"),
        P(None, "dp", None, "mp"),
        P("section", "dp", None, None),
        P(None, "dp", None, None),
        P(None, "dp", None),
        P(),
        P(None, "mp"),
        P(None, "mp"),
        P("section", None),
        P("section", None, "mp"),
        P("section", None, "mp"),
        P("section", None, "mp"),
        P("section", None, "mp"),
    )
    return jax.shard_map(
        on_device,
        mesh=mesh,
        in_specs=placed,
        out_specs=(P("section", None, "mp"), P("section", None, "mp")),
        check_vma=False,
    )
```

profile of v0, /device:TPU:0, one launch (start us, length us, event | category | flops | bytes accessed | tf_op | source)
XLA Modules:
  0.0 1101.6 jit_solution(5113289207940649873)
XLA Ops:
  16.3 80.0 %all-gather.10.cloned.1.call-done = bf16[1024,4096]{1,0:T(8,128)(2,1)} async-done(((bf16[1024,256]{1,0:T(8,128)(2,1)}), bf16[1024,4096]{1,0:T(8,128)(2,1)}) %all-gather.10.cloned.1.call-update) | async-done | bytes 8388624 | tf_op jit(solution)/shard_map/all_gather | solution.py:22
  96.3 6.7 fusion.104
  108.5 17.1 %all-to-all-done = bf16[16,256,128]{2,1,0:T(8,128)(2,1)S(1)} async-done(((bf16[16,256,128]{2,1,0:T(8,128)(2,1)}), bf16[16,256,128]{2,1,0:T(8,128)(2,1)S(1)}, u32[]{:S(2)}, u32[]{:S(2)}) %all-to-all-start) | async-done | bytes 1048608 | tf_op jit(solution)/shard_map/all_to_all | solution.py:142
  133.1 13.0 %all-to-all-done.1 = bf16[16,128,256]{2,1,0:T(8,128)(2,1)S(1)} async-done(((bf16[16,128,256]{2,1,0:T(8,128)(2,1)}), bf16[16,128,256]{2,1,0:T(8,128)(2,1)S(1)}, u32[]{:S(2)}, u32[]{:S(2)}) %all-to-all-start.1) | async-done | bytes 1048608 | tf_op jit(solution)/shard_map/all_to_all | solution.py:141
  148.1 6.3 all-gather.12.cloned.1.call-done
  156.6 184.6 %while.54 = (s32[]{:T(128)}, bf16[2048,896]{1,0:T(8,128)(2,1)}, bf16[32768,56]{0,1:T(8,128)(2,1)}, s32[]{:T(128)}, s32[]{:T(128)}, /*index=5*/s32[]{:T(128)}, s3...) while((s32[]{:T(128)}, bf16[2048,896]{1,0:T(8,128)(2,1)}, ...), condition=%wide.region_2.3_spmd, body=%wide.region_1.2_spmd.sunk | while | flops 26 | bytes 688530 | solution.py:125
  341.2 22.4 %gather_fusion = bf16[4096,896]{1,0:T(8,128)(2,1)} fusion(bf16[2048,896]{1,0:T(8,128)(2,1)} %get-tuple-element.835, s32[4096]{0:T(1024)S(1)} %broadcast_clamp_fusion), kind=kCustom, calls=%fused_computation | custom fusion | bytes 14696448 | tf_op jit(solution)/shard_map/jit(_take)/gather | solution.py:126
  385.3 318.6 %while.55 = (s32[]{:T(128)}, bf16[256,128]{1,0:T(8,128)(2,1)S(1)}, bf16[2,256,2048]{2,1,0:T(8,128)(2,1)}, pred[]{:T(512)}, s32[]{:T(128)}, /*index=5*/bf16[2,256...) while((s32[]{:T(128)}, bf16[256,128]{1,0:T(8,128)(2,1)S(1)}, ...), condition=%wide.region_8.9_spmd, body=%wide.region_3.8_spmd.sunk | while | flops 677446400 | bytes 32006564 | solution.py:175
  386.1 45.0 %all-gather.14.cloned.1.call-done = bf16[256,2048]{1,0:T(8,128)(2,1)} async-done(((bf16[256,128]{1,0:T(8,128)(2,1)}), bf16[256,2048]{1,0:T(8,128)(2,1)}) %all-gather.14.cloned.1.call-update) | async-done | bytes 1048592 | tf_op jit(solution)/shard_map/while/body/eval_jaxpr/all_gather | solution.py:22
  441.1 44.5 %all-gather.16.cloned.1.call-done = bf16[256,4096]{1,0:T(8,128)(2,1)} async-done(((bf16[256,256]{1,0:T(8,128)(2,1)}), bf16[256,4096]{1,0:T(8,128)(2,1)}) %all-gather.16.cloned.1.call-update) | async-done | bytes 2097168 | tf_op jit(solution)/shard_map/while/body/eval_jaxpr/all_gather | solution.py:22
  492.2 45.0 %all-gather.14.cloned.1.call-done = bf16[256,2048]{1,0:T(8,128)(2,1)} async-done(((bf16[256,128]{1,0:T(8,128)(2,1)}), bf16[256,2048]{1,0:T(8,128)(2,1)}) %all-gather.14.cloned.1.call-update) | async-done | bytes 1048592 | tf_op jit(solution)/shard_map/while/body/eval_jaxpr/all_gather | solution.py:22
  547.2 44.5 %all-gather.16.cloned.1.call-done = bf16[256,4096]{1,0:T(8,128)(2,1)} async-done(((bf16[256,256]{1,0:T(8,128)(2,1)}), bf16[256,4096]{1,0:T(8,128)(2,1)}) %all-gather.16.cloned.1.call-update) | async-done | bytes 2097168 | tf_op jit(solution)/shard_map/while/body/eval_jaxpr/all_gather | solution.py:22
  598.3 45.2 %all-gather.14.cloned.1.call-done = bf16[256,2048]{1,0:T(8,128)(2,1)} async-done(((bf16[256,128]{1,0:T(8,128)(2,1)}), bf16[256,2048]{1,0:T(8,128)(2,1)}) %all-gather.14.cloned.1.call-update) | async-done | bytes 1048592 | tf_op jit(solution)/shard_map/while/body/eval_jaxpr/all_gather | solution.py:22
  653.6 44.5 %all-gather.16.cloned.1.call-done = bf16[256,4096]{1,0:T(8,128)(2,1)} async-done(((bf16[256,256]{1,0:T(8,128)(2,1)}), bf16[256,4096]{1,0:T(8,128)(2,1)}) %all-gather.16.cloned.1.call-update) | async-done | bytes 2097168 | tf_op jit(solution)/shard_map/while/body/eval_jaxpr/all_gather | solution.py:22
  708.8 323.1 %while.56 = (s32[]{:T(128)}, bf16[256,128]{1,0:T(8,128)(2,1)S(1)}, bf16[2,4,512,2,128]{4,3,2,1,0:T(2,128)(2,1)}, bf16[2,4,512,2,128]{4,3,2,1,0:T(2,128)(2,1)}, p...) while((s32[]{:T(128)}, bf16[256,128]{1,0:T(8,128)(2,1)S(1)}, ...), condition=%wide.region_17.18_spmd, body=%wide.region_9.17_spmd.sunk | while | flops 1152261888 | bytes 76540544 | solution.py:216
  715.5 39.3 %all-gather.18.cloned.1.call-done = bf16[256,2048]{1,0:T(8,128)(2,1)} async-done(((bf16[256,128]{1,0:T(8,128)(2,1)}), bf16[256,2048]{1,0:T(8,128)(2,1)}) %all-gather.18.cloned.1.call-update) | async-done | bytes 1048592 | tf_op jit(solution)/shard_map/while/body/eval_jaxpr/all_gather | solution.py:22
  782.7 22.8 %all-gather.2 = bf16[16,1,256]{2,1,0:T(2,128)(2,1)S(1)} all-gather(bf16[1,1,256]{2,1,0:T(2,128)(2,1)S(1)} %reshape.462), channel_id=1, replica_groups=mesh['section'=2,'dp'=4,'mp'=16] {'mp'}, dimensions={0}, use_global_device_ids=true | all-gather | bytes 8704 | tf_op jit(solution)/shard_map/while/body/eval_jaxpr/all_gather | solution.py:28
  822.7 40.1 %all-gather.18.cloned.1.call-done = bf16[256,2048]{1,0:T(8,128)(2,1)} async-done(((bf16[256,128]{1,0:T(8,128)(2,1)}), bf16[256,2048]{1,0:T(8,128)(2,1)}) %all-gather.18.cloned.1.call-update) | async-done | bytes 1048592 | tf_op jit(solution)/shard_map/while/body/eval_jaxpr/all_gather | solution.py:22
  890.7 22.8 %all-gather.2 = bf16[16,1,256]{2,1,0:T(2,128)(2,1)S(1)} all-gather(bf16[1,1,256]{2,1,0:T(2,128)(2,1)S(1)} %reshape.462), channel_id=1, replica_groups=mesh['section'=2,'dp'=4,'mp'=16] {'mp'}, dimensions={0}, use_global_device_ids=true | all-gather | bytes 8704 | tf_op jit(solution)/shard_map/while/body/eval_jaxpr/all_gather | solution.py:28
  930.7 40.1 %all-gather.18.cloned.1.call-done = bf16[256,2048]{1,0:T(8,128)(2,1)} async-done(((bf16[256,128]{1,0:T(8,128)(2,1)}), bf16[256,2048]{1,0:T(8,128)(2,1)}) %all-gather.18.cloned.1.call-update) | async-done | bytes 1048592 | tf_op jit(solution)/shard_map/while/body/eval_jaxpr/all_gather | solution.py:22
  998.7 22.8 %all-gather.2 = bf16[16,1,256]{2,1,0:T(2,128)(2,1)S(1)} all-gather(bf16[1,1,256]{2,1,0:T(2,128)(2,1)S(1)} %reshape.462), channel_id=1, replica_groups=mesh['section'=2,'dp'=4,'mp'=16] {'mp'}, dimensions={0}, use_global_device_ids=true | all-gather | bytes 8704 | tf_op jit(solution)/shard_map/while/body/eval_jaxpr/all_gather | solution.py:28
  1031.9 7.4 fusion.101
  1039.3 6.7 fusion.98
  1046.1 45.3 %all-reduce.3.cloned.1.call-done = (bf16[1,896,256]{2,1,0:T(8,128)(2,1)}, bf16[1,896,256]{2,1,0:T(8,128)(2,1)}) async-done(((bf16[1,896,256]{2,1,0:T(8,128)(2,1)}, bf16[1,896,256]{2,1,0:T(8,128)(2,1)}), (bf16[1,896,256]{2,1,0:T(8,128)(2,1)}, bf16[1,896,256]{2,1,0:T(8,128)(2,1)})) %all-reduce.3.cloned.1.call-update) | async-done | bytes 917520 | tf_op jit(solution)/shard_map/psum | solution.py:233
  (378 shorter events, 424.3 us)
Async XLA Ops:
  7.2 356.4 %copy-start = (bf16[1,896,256]{2,1,0:T(8,128)(2,1)S(1)}, bf16[1,896,256]{2,1,0:T(8,128)(2,1)}, u32[]{:S(2)}) copy-start(bf16[1,896,256]{2,1,0:T(8,128)(2,1)} %param.35) | copy-start | bytes 1376260
  7.2 89.1 %all-gather.10.cloned.1.call-start = ((), (), s32[]{:S(2)}) async-start(), calls=%async_computation.2 | async-start | bytes 8912896 | tf_op jit(solution)/shard_map/all_gather | solution.py:22
  16.3 138.2 %all-gather.12.cloned.1.call-start = ((), (), s32[]{:S(2)}) async-start(), calls=%async_computation.3 | async-start | bytes 3784704 | tf_op jit(solution)/shard_map/all_gather | solution.py:116
  103.0 22.6 %all-to-all-start = ((bf16[16,256,128]{2,1,0:T(8,128)(2,1)}), bf16[16,256,128]{2,1,0:T(8,128)(2,1)S(1)}, u32[]{:S(2)}, u32[]{:S(2)}) async-start(bf16[16,256,128]{2,1,0:T(8,128)(2,1)} %bitcast.38), calls=%async_computation | async-start | bytes 2097152 | tf_op jit(solution)/shard_map/all_to_all | solution.py:142
  125.6 20.5 %all-to-all-start.1 = ((bf16[16,128,256]{2,1,0:T(8,128)(2,1)}), bf16[16,128,256]{2,1,0:T(8,128)(2,1)S(1)}, u32[]{:S(2)}, u32[]{:S(2)}) async-start(bf16[16,128,256]{2,1,0:T(8,128)(2,1)} %bitcast.41), calls=%async_computation.1 | async-start | bytes 2097152 | tf_op jit(solution)/shard_map/all_to_all | solution.py:141
  385.3 45.8 %all-gather.14.cloned.1.call-start = ((), (), s32[]{:S(2)}) async-start(), calls=%async_computation.5 | async-start | bytes 1114112 | tf_op jit(solution)/shard_map/while/body/eval_jaxpr/all_gather | solution.py:22
  386.0 99.5 %all-gather.16.cloned.1.call-start = ((), (), s32[]{:S(2)}) async-start(), calls=%async_computation.6 | async-start | bytes 2228224 | tf_op jit(solution)/shard_map/while/body/eval_jaxpr/all_gather | solution.py:22
  488.2 3.3 collective-permute-start
  491.5 45.7 %all-gather.14.cloned.1.call-start = ((), (), s32[]{:S(2)}) async-start(), calls=%async_computation.5 | async-start | bytes 1114112 | tf_op jit(solution)/shard_map/while/body/eval_jaxpr/all_gather | solution.py:22
  492.1 99.6 %all-gather.16.cloned.1.call-start = ((), (), s32[]{:S(2)}) async-start(), calls=%async_computation.6 | async-start | bytes 2228224 | tf_op jit(solution)/shard_map/while/body/eval_jaxpr/all_gather | solution.py:22
  594.2 3.3 collective-permute-start
  597.5 46.0 %all-gather.14.cloned.1.call-start = ((), (), s32[]{:S(2)}) async-start(), calls=%async_computation.5 | async-start | bytes 1114112 | tf_op jit(solution)/shard_map/while/body/eval_jaxpr/all_gather | solution.py:22
  598.3 99.8 %all-gather.16.cloned.1.call-start = ((), (), s32[]{:S(2)}) async-start(), calls=%async_computation.6 | async-start | bytes 2228224 | tf_op jit(solution)/shard_map/while/body/eval_jaxpr/all_gather | solution.py:22
  700.6 3.3 collective-permute-start
  708.8 46.0 %all-gather.18.cloned.1.call-start = ((), (), s32[]{:S(2)}) async-start(), calls=%async_computation.7 | async-start | bytes 1114112 | tf_op jit(solution)/shard_map/while/body/eval_jaxpr/all_gather | solution.py:22
  709.5 98.6 %all-gather.20.cloned.1.call-start = ((), (), s32[]{:S(2)}) async-start(), calls=%async_computation.8 | async-start | bytes 2228224 | tf_op jit(solution)/shard_map/while/body/eval_jaxpr/all_gather | solution.py:27
  810.8 3.8 collective-permute-start.1
  815.9 46.8 %all-gather.18.cloned.1.call-start = ((), (), s32[]{:S(2)}) async-start(), calls=%async_computation.7 | async-start | bytes 1114112 | tf_op jit(solution)/shard_map/while/body/eval_jaxpr/all_gather | solution.py:22
  816.7 99.4 %all-gather.20.cloned.1.call-start = ((), (), s32[]{:S(2)}) async-start(), calls=%async_computation.8 | async-start | bytes 2228224 | tf_op jit(solution)/shard_map/while/body/eval_jaxpr/all_gather | solution.py:27
  918.8 3.8 collective-permute-start.1
  923.9 46.8 %all-gather.18.cloned.1.call-start = ((), (), s32[]{:S(2)}) async-start(), calls=%async_computation.7 | async-start | bytes 1114112 | tf_op jit(solution)/shard_map/while/body/eval_jaxpr/all_gather | solution.py:22
  924.6 99.4 %all-gather.20.cloned.1.call-start = ((), (), s32[]{:S(2)}) async-start(), calls=%async_computation.8 | async-start | bytes 2228224 | tf_op jit(solution)/shard_map/while/body/eval_jaxpr/all_gather | solution.py:27
  1026.8 3.8 collective-permute-start.1
  1031.9 59.5 %all-reduce.3.cloned.1.call-start = ((), (), s32[]{:S(2)}) async-start(), calls=%async_computation.4 | async-start | bytes 1835008 | tf_op jit(solution)/shard_map/psum | solution.py:233
  (35 other events, 593.1 us)
Sparse Core Ops, SparseCore 0:
  16.4 79.8 all-gather.9
  103.2 51.2 all-gather.11
  388.8 42.2 all-gather.13
  439.2 46.3 all-gather.15
  494.6 42.4 all-gather.13
  545.2 46.3 all-gather.15
  601.0 42.5 all-gather.13
  651.6 46.3 all-gather.15
  712.3 42.5 all-gather.17
  761.7 46.3 all-gather.19
  819.4 43.2 all-gather.17
  869.6 46.3 all-gather.19
  927.4 43.3 all-gather.17
  977.6 46.3 all-gather.19
  1046.2 45.1 all-reduce.2
where the time goes:
time: 1110 us; the launch traced here: 1100 us
  waiting for transfers between devices  558 us (50%)
  local copies, waits for them, and re-layouts  296 us (27%)
  matrix products  120 us (11%)
  blocking collectives  68.5 us (6%)
  other arithmetic  26 us (2%)
  starting transfers between devices  17 us (2%)
  between operations  13.9 us (1%)
    all_gather x10, waiting for transfers between devices, collect(): return lax.all_gather(tensor, 'mp', axis=1, tiled=True)  468 us
    dynamic_update_slice x32, local copies, waits for them, and re-layouts, one_shard(): lax.dynamic_update_slice(whole_pool, shard_block, (row_start, col_start))  149 us
    all_gather x3, blocking collectives, collect_pair(): lax.all_gather(second, 'mp', axis=1, tiled=True)  68.5 us
    psum x1, waiting for transfers between devices, on_device(): lax.psum(key_sum.astype(jnp.bfloat16), 'dp').astype(jnp.float32)  45.3 us
    dynamic_slice x64, local copies, waits for them, and re-layouts, one_shard(): lax.dynamic_slice_in_dim(portion, position * shard_rows, shard_rows, 0)  34.4 us
    gather x1, local copies, waits for them, and re-layouts, on_device(): neighbours = jnp.take(whole_pool, global_rows, axis=0)  22.4 us
  transfers between devices with their start and end apart: 23, of which 17 were waited for; matrix products, arithmetic and copies ran while one was open for 10% of the time, Pallas kernels for 0%

commit v1 on v0

--- a/solution.py
+++ b/solution.py
@@ -2,10 +2,15 @@
 import jax.numpy as jnp
 from jax import lax
 from jax.sharding import PartitionSpec as P
+from jax.lax import all_gather
 
 HEAD = 128
 NT = 128
 EPSILON = 1e-05
+
+
+def play_strings(m):
+    return all_gather(m, "dp").sum(axis=0)
 
 
 def passed_along(value, axis, by):
@@ -230,7 +235,7 @@
         preferred_element_type=jnp.float32,
     )
     key_total, value_total = (
-        lax.psum(key_sum.astype(jnp.bfloat16), "dp").astype(jnp.float32),
+        play_strings(key_sum.astype(jnp.bfloat16)).astype(jnp.float32),
         lax.psum(value_sum.astype(jnp.bfloat16), "dp").astype(jnp.float32),
     )
     return (key_total.astype(jnp.bfloat16)[None], value_total.astype(jnp.bfloat16)[None])

time: 1110 us -> 1130 us (1.018)
  waiting for transfers between devices: 558 us -> 578 us
    all_gather x0 -> x1, waiting for transfers between devices: none -> 21.9 us  [play_strings(): return all_gather(m, 'dp').sum(axis=0)]
  transfers between devices with their start and end apart: 23 -> 24, of which waited for: 17 -> 18; matrix products, arithmetic and copies ran while one was open for 10% -> 10% of each run, Pallas kernels for 0% -> 0%
where the time goes in v1:
time: 1130 us; the launch traced here: 1120 us
  waiting for transfers between devices  578 us (51%)
  local copies, waits for them, and re-layouts  295 us (26%)
  matrix products  119 us (11%)
  blocking collectives  68.3 us (6%)
  other arithmetic  28.1 us (2%)
  starting transfers between devices  17.1 us (2%)
  between operations  14 us (1%)
    all_gather x10, waiting for transfers between devices, collect(): return lax.all_gather(tensor, 'mp', axis=1, tiled=True)  468 us
    dynamic_update_slice x32, local copies, waits for them, and re-layouts, one_shard(): lax.dynamic_update_slice(whole_pool, shard_block, (row_start, col_start))  149 us
    all_gather x3, blocking collectives, collect_pair(): lax.all_gather(second, 'mp', axis=1, tiled=True)  68.3 us
    psum x1, waiting for transfers between devices, on_device(): lax.psum(value_sum.astype(jnp.bfloat16), 'dp').astype(jnp.float32)  42 us
    dynamic_slice x64, local copies, waits for them, and re-layouts, one_shard(): lax.dynamic_slice_in_dim(portion, position * shard_rows, shard_rows, 0)  34.4 us
  transfers between devices with their start and end apart: 24, of which 18 were waited for; matrix products, arithmetic and copies ran while one was open for 10% of the time, Pallas kernels for 0%

profile of v1, /device:TPU:0, one launch (start us, length us, event | category | flops | bytes accessed | tf_op | source)
XLA Modules:
  0.0 1121.5 jit_solution(8041011149730678347)
XLA Ops:
  16.3 80.0 %all-gather.12.cloned.1.call-done = bf16[1024,4096]{1,0:T(8,128)(2,1)} async-done(((bf16[1024,256]{1,0:T(8,128)(2,1)}), bf16[1024,4096]{1,0:T(8,128)(2,1)}) %all-gather.12.cloned.1.call-update) | async-done | bytes 8388624 | tf_op jit(solution)/shard_map/all_gather | solution.py:27
  96.3 6.7 fusion.101
  108.5 17.1 %all-to-all-done = bf16[16,256,128]{2,1,0:T(8,128)(2,1)S(1)} async-done(((bf16[16,256,128]{2,1,0:T(8,128)(2,1)}), bf16[16,256,128]{2,1,0:T(8,128)(2,1)S(1)}, u32[]{:S(2)}, u32[]{:S(2)}) %all-to-all-start) | async-done | bytes 1048608 | tf_op jit(solution)/shard_map/all_to_all | solution.py:147
  133.1 13.0 %all-to-all-done.1 = bf16[16,128,256]{2,1,0:T(8,128)(2,1)S(1)} async-done(((bf16[16,128,256]{2,1,0:T(8,128)(2,1)}), bf16[16,128,256]{2,1,0:T(8,128)(2,1)S(1)}, u32[]{:S(2)}, u32[]{:S(2)}) %all-to-all-start.1) | async-done | bytes 1048608 | tf_op jit(solution)/shard_map/all_to_all | solution.py:146
  156.6 185.1 %while.54 = (s32[]{:T(128)}, bf16[2048,896]{1,0:T(8,128)(2,1)}, bf16[32768,56]{0,1:T(8,128)(2,1)}, s32[]{:T(128)}, s32[]{:T(128)}, /*index=5*/s32[]{:T(128)}, s3...) while((s32[]{:T(128)}, bf16[2048,896]{1,0:T(8,128)(2,1)}, ...), condition=%wide.region_2.3_spmd, body=%wide.region_1.2_spmd.sunk | while | flops 26 | bytes 688530 | solution.py:130
  341.7 22.4 %gather_fusion = bf16[4096,896]{1,0:T(8,128)(2,1)} fusion(bf16[2048,896]{1,0:T(8,128)(2,1)} %get-tuple-element.835, s32[4096]{0:T(1024)S(1)} %broadcast_clamp_fusion), kind=kCustom, calls=%fused_computation | custom fusion | bytes 14696448 | tf_op jit(solution)/shard_map/jit(_take)/gather | solution.py:131
  385.8 318.4 %while.55 = (s32[]{:T(128)}, bf16[256,128]{1,0:T(8,128)(2,1)S(1)}, bf16[2,256,2048]{2,1,0:T(8,128)(2,1)}, pred[]{:T(512)}, s32[]{:T(128)}, /*index=5*/bf16[2,256...) while((s32[]{:T(128)}, bf16[256,128]{1,0:T(8,128)(2,1)S(1)}, ...), condition=%wide.region_8.9_spmd, body=%wide.region_3.8_spmd.sunk | while | flops 677446400 | bytes 32006564 | solution.py:180
  386.6 45.0 %all-gather.18.cloned.1.call-done = bf16[256,2048]{1,0:T(8,128)(2,1)} async-done(((bf16[256,128]{1,0:T(8,128)(2,1)}), bf16[256,2048]{1,0:T(8,128)(2,1)}) %all-gather.18.cloned.1.call-update) | async-done | bytes 1048592 | tf_op jit(solution)/shard_map/while/body/eval_jaxpr/all_gather | solution.py:27
  441.6 44.5 %all-gather.20.cloned.1.call-done = bf16[256,4096]{1,0:T(8,128)(2,1)} async-done(((bf16[256,256]{1,0:T(8,128)(2,1)}), bf16[256,4096]{1,0:T(8,128)(2,1)}) %all-gather.20.cloned.1.call-update) | async-done | bytes 2097168 | tf_op jit(solution)/shard_map/while/body/eval_jaxpr/all_gather | solution.py:27
  492.7 45.0 %all-gather.18.cloned.1.call-done = bf16[256,2048]{1,0:T(8,128)(2,1)} async-done(((bf16[256,128]{1,0:T(8,128)(2,1)}), bf16[256,2048]{1,0:T(8,128)(2,1)}) %all-gather.18.cloned.1.call-update) | async-done | bytes 1048592 | tf_op jit(solution)/shard_map/while/body/eval_jaxpr/all_gather | solution.py:27
  547.6 44.5 %all-gather.20.cloned.1.call-done = bf16[256,4096]{1,0:T(8,128)(2,1)} async-done(((bf16[256,256]{1,0:T(8,128)(2,1)}), bf16[256,4096]{1,0:T(8,128)(2,1)}) %all-gather.20.cloned.1.call-update) | async-done | bytes 2097168 | tf_op jit(solution)/shard_map/while/body/eval_jaxpr/all_gather | solution.py:27
  598.7 45.2 %all-gather.18.cloned.1.call-done = bf16[256,2048]{1,0:T(8,128)(2,1)} async-done(((bf16[256,128]{1,0:T(8,128)(2,1)}), bf16[256,2048]{1,0:T(8,128)(2,1)}) %all-gather.18.cloned.1.call-update) | async-done | bytes 1048592 | tf_op jit(solution)/shard_map/while/body/eval_jaxpr/all_gather | solution.py:27
  653.9 44.5 %all-gather.20.cloned.1.call-done = bf16[256,4096]{1,0:T(8,128)(2,1)} async-done(((bf16[256,256]{1,0:T(8,128)(2,1)}), bf16[256,4096]{1,0:T(8,128)(2,1)}) %all-gather.20.cloned.1.call-update) | async-done | bytes 2097168 | tf_op jit(solution)/shard_map/while/body/eval_jaxpr/all_gather | solution.py:27
  709.1 323.1 %while.56 = (s32[]{:T(128)}, bf16[256,128]{1,0:T(8,128)(2,1)S(1)}, bf16[2,4,512,2,128]{4,3,2,1,0:T(2,128)(2,1)}, bf16[2,4,512,2,128]{4,3,2,1,0:T(2,128)(2,1)}, p...) while((s32[]{:T(128)}, bf16[256,128]{1,0:T(8,128)(2,1)S(1)}, ...), condition=%wide.region_17.18_spmd, body=%wide.region_9.17_spmd.sunk | while | flops 1152261888 | bytes 76540544 | solution.py:221
  715.8 39.3 %all-gather.22.cloned.1.call-done = bf16[256,2048]{1,0:T(8,128)(2,1)} async-done(((bf16[256,128]{1,0:T(8,128)(2,1)}), bf16[256,2048]{1,0:T(8,128)(2,1)}) %all-gather.22.cloned.1.call-update) | async-done | bytes 1048592 | tf_op jit(solution)/shard_map/while/body/eval_jaxpr/all_gather | solution.py:27
  782.7 22.8 %all-gather.3 = bf16[16,1,256]{2,1,0:T(2,128)(2,1)S(1)} all-gather(bf16[1,1,256]{2,1,0:T(2,128)(2,1)S(1)} %reshape.463), channel_id=1, replica_groups=mesh['section'=2,'dp'=4,'mp'=16] {'mp'}, dimensions={0}, use_global_device_ids=true | all-gather | bytes 8704 | tf_op jit(solution)/shard_map/while/body/eval_jaxpr/all_gather | solution.py:33
  823.0 40.1 %all-gather.22.cloned.1.call-done = bf16[256,2048]{1,0:T(8,128)(2,1)} async-done(((bf16[256,128]{1,0:T(8,128)(2,1)}), bf16[256,2048]{1,0:T(8,128)(2,1)}) %all-gather.22.cloned.1.call-update) | async-done | bytes 1048592 | tf_op jit(solution)/shard_map/while/body/eval_jaxpr/all_gather | solution.py:27
  890.7 22.8 %all-gather.3 = bf16[16,1,256]{2,1,0:T(2,128)(2,1)S(1)} all-gather(bf16[1,1,256]{2,1,0:T(2,128)(2,1)S(1)} %reshape.463), channel_id=1, replica_groups=mesh['section'=2,'dp'=4,'mp'=16] {'mp'}, dimensions={0}, use_global_device_ids=true | all-gather | bytes 8704 | tf_op jit(solution)/shard_map/while/body/eval_jaxpr/all_gather | solution.py:33
  931.0 40.1 %all-gather.22.cloned.1.call-done = bf16[256,2048]{1,0:T(8,128)(2,1)} async-done(((bf16[256,128]{1,0:T(8,128)(2,1)}), bf16[256,2048]{1,0:T(8,128)(2,1)}) %all-gather.22.cloned.1.call-update) | async-done | bytes 1048592 | tf_op jit(solution)/shard_map/while/body/eval_jaxpr/all_gather | solution.py:27
  998.6 22.8 %all-gather.3 = bf16[16,1,256]{2,1,0:T(2,128)(2,1)S(1)} all-gather(bf16[1,1,256]{2,1,0:T(2,128)(2,1)S(1)} %reshape.463), channel_id=1, replica_groups=mesh['section'=2,'dp'=4,'mp'=16] {'mp'}, dimensions={0}, use_global_device_ids=true | all-gather | bytes 8704 | tf_op jit(solution)/shard_map/while/body/eval_jaxpr/all_gather | solution.py:33
  1032.2 7.4 fusion.92
  1039.7 6.7 fusion.98
  1046.5 21.9 %all-gather.16.cloned.1.call-done = bf16[3584,256]{1,0:T(8,128)(2,1)} async-done(((bf16[896,256]{1,0:T(8,128)(2,1)}), bf16[3584,256]{1,0:T(8,128)(2,1)}) %all-gather.16.cloned.1.call-update) | async-done | bytes 1835024 | tf_op jit(solution)/shard_map/all_gather | solution.py:13
  1071.1 42.0 %all-reduce.2.cloned.1.call-done = bf16[1,896,256]{2,1,0:T(8,128)(2,1)} async-done(((bf16[1,896,256]{2,1,0:T(8,128)(2,1)}), bf16[1,896,256]{2,1,0:T(8,128)(2,1)}) %all-reduce.2.cloned.1.call-update) | async-done | bytes 458768 | tf_op jit(solution)/shard_map/psum | solution.py:239
  (381 shorter events, 431.5 us)
Async XLA Ops:
  7.2 89.1 %all-gather.12.cloned.1.call-start = ((), (), s32[]{:S(2)}) async-start(), calls=%async_computation.2 | async-start | bytes 8912896 | tf_op jit(solution)/shard_map/all_gather | solution.py:27
  16.3 138.2 %all-gather.14.cloned.1.call-start = ((), (), s32[]{:S(2)}) async-start(), calls=%async_computation.3 | async-start | bytes 3784704 | tf_op jit(solution)/shard_map/all_gather | solution.py:121
  103.0 22.6 %all-to-all-start = ((bf16[16,256,128]{2,1,0:T(8,128)(2,1)}), bf16[16,256,128]{2,1,0:T(8,128)(2,1)S(1)}, u32[]{:S(2)}, u32[]{:S(2)}) async-start(bf16[16,256,128]{2,1,0:T(8,128)(2,1)} %bitcast.38), calls=%async_computation | async-start | bytes 2097152 | tf_op jit(solution)/shard_map/all_to_all | solution.py:147
  125.6 20.5 %all-to-all-start.1 = ((bf16[16,128,256]{2,1,0:T(8,128)(2,1)}), bf16[16,128,256]{2,1,0:T(8,128)(2,1)S(1)}, u32[]{:S(2)}, u32[]{:S(2)}) async-start(bf16[16,128,256]{2,1,0:T(8,128)(2,1)} %bitcast.41), calls=%async_computation.1 | async-start | bytes 2097152 | tf_op jit(solution)/shard_map/all_to_all | solution.py:146
  385.8 45.8 %all-gather.18.cloned.1.call-start = ((), (), s32[]{:S(2)}) async-start(), calls=%async_computation.6 | async-start | bytes 1114112 | tf_op jit(solution)/shard_map/while/body/eval_jaxpr/all_gather | solution.py:27
  386.5 99.5 %all-gather.20.cloned.1.call-start = ((), (), s32[]{:S(2)}) async-start(), calls=%async_computation.7 | async-start | bytes 2228224 | tf_op jit(solution)/shard_map/while/body/eval_jaxpr/all_gather | solution.py:27
  488.6 3.3 collective-permute-start
  491.9 45.7 %all-gather.18.cloned.1.call-start = ((), (), s32[]{:S(2)}) async-start(), calls=%async_computation.6 | async-start | bytes 1114112 | tf_op jit(solution)/shard_map/while/body/eval_jaxpr/all_gather | solution.py:27
  492.6 99.6 %all-gather.20.cloned.1.call-start = ((), (), s32[]{:S(2)}) async-start(), calls=%async_computation.7 | async-start | bytes 2228224 | tf_op jit(solution)/shard_map/while/body/eval_jaxpr/all_gather | solution.py:27
  594.7 3.2 collective-permute-start
  597.9 46.0 %all-gather.18.cloned.1.call-start = ((), (), s32[]{:S(2)}) async-start(), calls=%async_computation.6 | async-start | bytes 1114112 | tf_op jit(solution)/shard_map/while/body/eval_jaxpr/all_gather | solution.py:27
  598.7 99.8 %all-gather.20.cloned.1.call-start = ((), (), s32[]{:S(2)}) async-start(), calls=%async_computation.7 | async-start | bytes 2228224 | tf_op jit(solution)/shard_map/while/body/eval_jaxpr/all_gather | solution.py:27
  701.0 3.2 collective-permute-start
  709.1 46.0 %all-gather.22.cloned.1.call-start = ((), (), s32[]{:S(2)}) async-start(), calls=%async_computation.8 | async-start | bytes 1114112 | tf_op jit(solution)/shard_map/while/body/eval_jaxpr/all_gather | solution.py:27
  709.8 98.6 %all-gather.24.cloned.1.call-start = ((), (), s32[]{:S(2)}) async-start(), calls=%async_computation.9 | async-start | bytes 2228224 | tf_op jit(solution)/shard_map/while/body/eval_jaxpr/all_gather | solution.py:32
  811.1 3.8 collective-permute-start.1
  816.3 46.8 %all-gather.22.cloned.1.call-start = ((), (), s32[]{:S(2)}) async-start(), calls=%async_computation.8 | async-start | bytes 1114112 | tf_op jit(solution)/shard_map/while/body/eval_jaxpr/all_gather | solution.py:27
  817.0 99.4 %all-gather.24.cloned.1.call-start = ((), (), s32[]{:S(2)}) async-start(), calls=%async_computation.9 | async-start | bytes 2228224 | tf_op jit(solution)/shard_map/while/body/eval_jaxpr/all_gather | solution.py:32
  919.1 3.8 collective-permute-start.1
  924.2 46.8 %all-gather.22.cloned.1.call-start = ((), (), s32[]{:S(2)}) async-start(), calls=%async_computation.8 | async-start | bytes 1114112 | tf_op jit(solution)/shard_map/while/body/eval_jaxpr/all_gather | solution.py:27
  925.0 99.4 %all-gather.24.cloned.1.call-start = ((), (), s32[]{:S(2)}) async-start(), calls=%async_computation.9 | async-start | bytes 2228224 | tf_op jit(solution)/shard_map/while/body/eval_jaxpr/all_gather | solution.py:32
  1027.1 3.8 collective-permute-start.1
  1032.2 36.2 %all-gather.16.cloned.1.call-start = ((), (), s32[]{:S(2)}) async-start(), calls=%async_computation.5 | async-start | bytes 2293760 | tf_op jit(solution)/shard_map/all_gather | solution.py:13
  1039.6 73.5 %all-reduce.2.cloned.1.call-start = ((), (), s32[]{:S(2)}) async-start(), calls=%async_computation.4 | async-start | bytes 917504 | tf_op jit(solution)/shard_map/psum | solution.py:239
  (36 other events, 970.3 us)
Sparse Core Ops, SparseCore 0:
  16.4 79.8 all-gather.11
  103.2 51.2 all-gather.13
  389.3 42.2 all-gather.17
  439.7 46.3 all-gather.19
  495.1 42.5 all-gather.17
  545.7 46.3 all-gather.19
  601.4 42.5 all-gather.17
  652.0 46.3 all-gather.19
  712.6 42.5 all-gather.21
  762.0 46.4 all-gather.23
  819.7 43.2 all-gather.21
  869.9 46.3 all-gather.23
  927.7 43.2 all-gather.21
  977.9 46.4 all-gather.23
  1039.8 28.5 all-gather.15
  1070.6 42.4 all-reduce.1
